TPU v7x, 512 devices: a whole 4x8x8 slice. The times are simulated.
512 devices in a mesh: dp: 64 (over z_hi, y, core), rows: 8 (over z_lo, x).
Axes of the slice: x: 4, y: 8, z: 8 (z_hi: 4, z_lo: 2; z = z_hi * 2 + z_lo), core: 2. Of those that a mesh axis runs over, the one named last changes fastest.
Arguments:
- latents: bfloat16 [64, 32, 32, 640], P('dp', 'rows'), may hold values from -6 to 6
- target: bfloat16 [64, 32, 32, 640], P('dp', 'rows'), may hold values from -6 to 6
- weight: float32 [9, 640, 640], P(None, 'rows', 'dp'), may hold values from -0.078125 to 0.078125
- moment1: float32 [9, 640, 640], P(None, 'rows', 'dp'), may hold values from -6 to 6
- moment2: float32 [9, 640, 640], P(None, 'rows', 'dp'), may hold values from 0.5 to 4
Outputs:
- student: bfloat16 [64, 32, 32, 640], P('dp', 'rows')
- input_grad: bfloat16 [64, 32, 32, 640], P('dp', 'rows')
- new_weight: float32 [9, 640, 640], P(None, 'rows', 'dp')
- new_moment1: float32 [9, 640, 640], P(None, 'rows', 'dp')
- new_moment2: float32 [9, 640, 640], P(None, 'rows', 'dp')
All inputs are finite; a program needn't handle non-finite values.
Results may differ from a plain program's by a relative error of at most 0.009.
Values may be sent and summed in bfloat16 or wider, within the bound.
A program may use at most 128 MiB of HBM per device.

v0:
```python
import jax
import jax.numpy as jnp
from jax import lax
from jax.sharding import PartitionSpec as P


def per_device(latents, target, weight, moment1, moment2):
    n_rows = lax.axis_size("rows")
    n_dp = lax.axis_size("dp")
    batch, band, width, ch = latents.shape
    taps, cs, ns = weight.shape
    height = band * n_rows
    cells = batch * band * width
    own = weight.astype(jnp.bfloat16).transpose(2, 0, 1).reshape(ns, taps * cs)
    kernel = lax.all_gather(own, "dp", axis=0, tiled=True)
    x = lax.all_to_all(latents, "rows", split_axis=3, concat_axis=1, tiled=True)
    pad = jnp.pad(x, ((0, 0), (1, 1), (1, 1), (0, 0)))
    wins = [pad[:, a : a + height, c : c + width] for a in range(3) for c in range(3)]
    x9 = jnp.concatenate(wins, axis=-1).reshape(batch * height * width, taps * cs)
    part = lax.dot_general(x9, kernel, (((1,), (1,)), ((), ())), preferred_element_type=jnp.float32)
    part = part.astype(jnp.bfloat16).reshape(batch, n_rows, band * width, ch)
    part = part.transpose(1, 0, 2, 3).reshape(n_rows, cells, ch)
    part = lax.all_to_all(part, "rows", 0, 0, tiled=True)
    student = jnp.sum(part.astype(jnp.float32), axis=0).astype(jnp.bfloat16)
    error = student.astype(jnp.float32) - target.reshape(cells, ch).astype(jnp.float32)
    error = error.astype(jnp.bfloat16).reshape(batch, band, width, ch)
    err = lax.all_gather(error, "rows", axis=1, tiled=True).reshape(-1, ch)
    grad = lax.dot_general(err, x9, (((0,), (0,)), ((), ())), preferred_element_type=jnp.float32)
    grad = grad.astype(jnp.bfloat16).reshape(n_dp, ns, taps * cs)
    grad = lax.all_to_all(grad, "dp", 0, 0, tiled=True)
    grad = jnp.sum(grad.astype(jnp.float32), axis=0) / jnp.float32(batch * n_dp)
    grad = grad.reshape(ns, taps, cs).transpose(1, 2, 0)
    back = jnp.dot(err, kernel, preferred_element_type=jnp.float32)
    back = back.reshape(batch, height, width, taps, cs)
    back = jnp.pad(back, ((0, 0), (1, 1), (1, 1), (0, 0), (0, 0)))
    total = None
    for tap in range(taps):
        a, c = divmod(tap, 3)
        term = back[:, 2 - a : 2 - a + height, 2 - c : 2 - c + width, tap]
        total = term if total is None else total + term
    input_grad = lax.all_to_all(
        total.astype(jnp.bfloat16), "rows", split_axis=1, concat_axis=3, tiled=True
    )
    new_moment1 = 0.9 * moment1 + 0.1 * grad
    new_moment2 = 0.999 * moment2 + 0.001 * grad * grad
    new_weight = weight - 0.01 * new_moment1 / (jnp.sqrt(new_moment2) + 1e-08)
    return (student.reshape(latents.shape), input_grad, new_weight, new_moment1, new_moment2)


def solution(mesh):
    act = P("dp", "rows", None, None)
    par = P(None, "rows", "dp")
    return jax.shard_map(
        per_device,
        mesh=mesh,
        in_specs=(act, act, par, par, par),
        out_specs=(act, act, par, par, par),
        check_vma=False,
    )
```

profile of v0, /device:TPU:1, one launch (start us, length us, event | category | flops | bytes accessed | tf_op | source)
XLA Modules:
  0.0 255.2 jit_solution(7276642183336504303)
XLA Ops:
  7.2 1.3 copy.23
  8.5 1.3 reshape.187
  9.8 6.6 %all-to-all-start = ((bf16[8,2,5120]{2,1,0:T(2,128)(2,1)}), bf16[8,2,5120]{2,1,0:T(2,128)(2,1)S(1)}, u32[]{:S(2)}, u32[]{:S(2)}) async-start(bf16[8,2,5120]{2,1,0:T(2,128)(2,1)} %reshape.187), calls=%async_computation | async-start | bytes 327680 | tf_op jit(solution)/shard_map/all_to_all | solution.py:16
  16.5 0.1 reshape.181
  16.6 92.6 %all-gather = bf16[64,10,720]{2,1,0:T(8,128)(2,1)S(1)} all-gather(bf16[1,10,720]{2,1,0:T(8,128)(2,1)S(1)} %reshape.181), channel_id=1, replica_groups=mesh['dp'=64,'rows'=8] {'dp'}, dimensions={0}, use_global_device_ids=true | all-gather | bytes 936000 | tf_op jit(solution)/shard_map/all_gather | solution.py:15
  109.2 0.6 reshape.182
  109.8 0.3 reshape.188
  110.2 0.3 copy.24
  110.5 0.3 pad_slice_fusion.8
  110.9 2.4 concatenate.33
  113.3 2.8 %convolution_convert_fusion = bf16[1024,640]{1,0:T(8,128)(2,1)S(1)} fusion(bf16[1024,720]{1,0:T(8,128)(2,1)} %concatenate.33, bf16[640,720]{1,0:T(8,128)(2,1)S(1)} %reshape.182), kind=kOutput, calls=%fused_computation.11 | convolution fusion | flops 944373760 | bytes 3706880 | tf_op jit(solution)/shard_map/dot_general | solution.py:20
  116.2 23.0 %all_to_all.46 = bf16[8,128,640]{2,1,0:T(8,128)(2,1)S(1)} all-to-all(bf16[8,128,640]{2,1,0:T(8,128)(2,1)S(1)} %bitcast.78), channel_id=1, replica_groups=mesh['dp'=64,'rows'=8] {'rows'}, dimensions={0} | all-to-all | bytes 2621440 | tf_op jit(solution)/shard_map/all_to_all | solution.py:23
  139.2 0.2 reduce_sum.21
  139.4 1.7 subtract_convert_fusion
  141.2 1.3 copy.27
  142.6 2.4 concatenate.34
  145.0 26.3 %all-gather.3.cloned.1.call-done = bf16[1,32,32,640]{3,2,0,1:T(8,128)(2,1)} async-done(((bf16[1,4,32,640]{3,2,0,1:T(8,128)(2,1)}), bf16[1,32,32,640]{3,2,0,1:T(8,128)(2,1)}) %all-gather.3.cloned.1.call-update) | async-done | bytes 1310736 | tf_op jit(solution)/shard_map/all_gather | solution.py:27
  171.3 3.5 %convolution_bitcast_fusion = f32[1,32,32,9,80]{4,2,3,1,0:T(8,128)S(1)} fusion(bf16[9,80,640,1]{2,1,0,3:T(8,128)(2,1)S(1)} %bitcast.80, bf16[1,32,32,640]{3,2,0,1:T(8,128)(2,1)} %all-gather.3.cloned.1.call-done), kind=kOutput, calls=%fused_computation.9 | convolution fusion | flops 943718400 | bytes 5181440 | tf_op jit(solution)/shard_map/dot_general | solution.py:33
  174.8 1.3 fusion.15
  176.1 3.4 %all-to-all-start.2 = ((bf16[1,32,32,80]{3,2,0,1:T(8,128)(2,1)}), bf16[1,32,32,80]{3,2,0,1:T(8,128)(2,1)S(1)}, u32[]{:S(2)}, u32[]{:S(2)}) async-start(bf16[1,32,32,80]{3,2,0,1:T(8,128)(2,1)} %fusion.15), calls=%async_computation.2 | async-start | bytes 524288 | tf_op jit(solution)/shard_map/all_to_all | solution.py:41
  179.5 2.7 %bitcast_convert_fusion = bf16[640,720]{0,1:T(8,128)(2,1)S(1)} fusion(bf16[1,32,32,720]{3,2,1,0:T(8,128)(2,1)S(1)} %copy-done.10, bf16[1,32,32,640]{3,2,0,1:T(8,128)(2,1)} %all-gather.3.cloned.1.call-done), kind=kOutput, calls=%fused_computation.10 | convolution fusion | flops 944179200 | bytes 3706880 | tf_op jit(solution)/shard_map/dot_general | solution.py:28
  182.2 1.0 copy.31
  183.2 1.4 reshape.175
  184.6 1.0 all-to-all-done.2
  185.6 19.8 %all-to-all-start.3 = ((bf16[64,10,720]{2,1,0:T(8,128)(2,1)}), bf16[64,10,720]{2,1,0:T(8,128)(2,1)S(1)}, u32[]{:S(2)}, u32[]{:S(2)}) async-start(bf16[64,10,720]{2,1,0:T(8,128)(2,1)} %reshape.175), calls=%async_computation.3 | async-start | bytes 3145728 | tf_op jit(solution)/shard_map/all_to_all | solution.py:30
  205.4 0.2 copy.29
  205.6 0.9 all_to_all.40
  206.5 39.4 %all-to-all-done.3 = bf16[64,10,720]{2,1,0:T(8,128)(2,1)S(1)} async-done(((bf16[64,10,720]{2,1,0:T(8,128)(2,1)}), bf16[64,10,720]{2,1,0:T(8,128)(2,1)S(1)}, u32[]{:S(2)}, u32[]{:S(2)}) %all-to-all-start.3) | async-done | bytes 921632 | tf_op jit(solution)/shard_map/all_to_all | solution.py:30
  245.9 0.3 convert_reduce_fusion
  246.4 0.6 copy.35
  247.0 0.6 copy.36
  247.7 0.6 copy.37
  (42 shorter events, 0.3 us)
Async XLA Ops:
  7.2 9.3 %copy-start.13 = (f32[9,80,10]{1,2,0:T(8,128)S(1)}, f32[9,80,10]{1,2,0:T(8,128)}, u32[]{:S(2)}) copy-start(f32[9,80,10]{1,2,0:T(8,128)} %param.7) | copy-start | bytes 86404
  9.8 100.0 %all-to-all-start = ((bf16[8,2,5120]{2,1,0:T(2,128)(2,1)}), bf16[8,2,5120]{2,1,0:T(2,128)(2,1)S(1)}, u32[]{:S(2)}, u32[]{:S(2)}) async-start(bf16[8,2,5120]{2,1,0:T(2,128)(2,1)} %reshape.187), calls=%async_computation | async-start | bytes 327680 | tf_op jit(solution)/shard_map/all_to_all | solution.py:16
  16.4 154.8 %all-gather.3.cloned.1.call-start = ((), (), s32[]{:S(2)}) async-start(), calls=%async_computation.4 | async-start | bytes 1474560 | tf_op jit(solution)/shard_map/all_gather | solution.py:27
  110.8 2.5 copy-start
  110.8 2.5 copy-start.2
  110.8 2.5 copy-start.4
  110.8 2.5 copy-start.6
  110.9 2.5 copy-start.8
  139.4 5.6 %copy-start.12 = (bf16[128,640]{1,0:T(8,128)(2,1)}, bf16[128,640]{1,0:T(8,128)(2,1)S(1)}, u32[]{:S(2)}) copy-start(bf16[128,640]{1,0:T(8,128)(2,1)S(1)} %reduce_sum.21) | copy-start | bytes 491524
  139.4 3.1 %copy-start.1 = (bf16[1,32,32,80]{3,2,1,0:T(8,128)(2,1)S(1)}, bf16[1,32,32,80]{3,2,1,0:T(8,128)(2,1)}, u32[]{:S(2)}) copy-start(bf16[1,32,32,80]{3,2,1,0:T(8,128)(2,1)} %copy-done) | copy-start | bytes 491524
  139.4 3.1 %copy-start.3 = (bf16[1,32,32,80]{3,2,1,0:T(8,128)(2,1)S(1)}, bf16[1,32,32,80]{3,2,1,0:T(8,128)(2,1)}, u32[]{:S(2)}) copy-start(bf16[1,32,32,80]{3,2,1,0:T(8,128)(2,1)} %copy-done.2) | copy-start | bytes 491524
  139.4 3.1 %copy-start.5 = (bf16[1,32,32,80]{3,2,1,0:T(8,128)(2,1)S(1)}, bf16[1,32,32,80]{3,2,1,0:T(8,128)(2,1)}, u32[]{:S(2)}) copy-start(bf16[1,32,32,80]{3,2,1,0:T(8,128)(2,1)} %copy-done.4) | copy-start | bytes 491524
  139.4 3.1 %copy-start.7 = (bf16[1,32,32,80]{3,2,1,0:T(8,128)(2,1)S(1)}, bf16[1,32,32,80]{3,2,1,0:T(8,128)(2,1)}, u32[]{:S(2)}) copy-start(bf16[1,32,32,80]{3,2,1,0:T(8,128)(2,1)} %copy-done.6) | copy-start | bytes 491524
  139.4 3.1 %copy-start.9 = (bf16[1,32,32,80]{3,2,1,0:T(8,128)(2,1)S(1)}, bf16[1,32,32,80]{3,2,1,0:T(8,128)(2,1)}, u32[]{:S(2)}) copy-start(bf16[1,32,32,80]{3,2,1,0:T(8,128)(2,1)} %copy-done.8) | copy-start | bytes 491524
  142.6 28.7 %copy-start.11 = (bf16[720,640]{1,0:T(8,128)(2,1)S(1)}, bf16[720,640]{1,0:T(8,128)(2,1)}, u32[]{:S(2)}) copy-start(bf16[720,640]{1,0:T(8,128)(2,1)} %copy.27) | copy-start | bytes 2764804
  174.8 4.7 %copy-start.10 = (bf16[1,32,32,720]{3,2,1,0:T(8,128)(2,1)S(1)}, bf16[1,32,32,720]{3,2,1,0:T(8,128)(2,1)}, u32[]{:S(2)}) copy-start(bf16[1,32,32,720]{3,2,1,0:T(8,128)(2,1)} %concatenate.34) | copy-start | bytes 4423684
  176.1 9.5 %all-to-all-start.2 = ((bf16[1,32,32,80]{3,2,0,1:T(8,128)(2,1)}), bf16[1,32,32,80]{3,2,0,1:T(8,128)(2,1)S(1)}, u32[]{:S(2)}, u32[]{:S(2)}) async-start(bf16[1,32,32,80]{3,2,0,1:T(8,128)(2,1)} %fusion.15), calls=%async_computation.2 | async-start | bytes 524288 | tf_op jit(solution)/shard_map/all_to_all | solution.py:41
  185.6 60.3 %all-to-all-start.3 = ((bf16[64,10,720]{2,1,0:T(8,128)(2,1)}), bf16[64,10,720]{2,1,0:T(8,128)(2,1)S(1)}, u32[]{:S(2)}, u32[]{:S(2)}) async-start(bf16[64,10,720]{2,1,0:T(8,128)(2,1)} %reshape.175), calls=%async_computation.3 | async-start | bytes 3145728 | tf_op jit(solution)/shard_map/all_to_all | solution.py:30
  205.4 40.9 %copy-start.14 = (f32[9,80,10]{1,2,0:T(8,128)S(1)}, f32[9,80,10]{1,2,0:T(8,128)}, u32[]{:S(2)}) copy-start(f32[9,80,10]{1,2,0:T(8,128)} %param.7) | copy-start | bytes 86404
  205.4 40.9 %copy-start.15 = (f32[9,80,10]{1,2,0:T(8,128)S(1)}, f32[9,80,10]{1,2,0:T(8,128)}, u32[]{:S(2)}) copy-start(f32[9,80,10]{1,2,0:T(8,128)} %param.8) | copy-start | bytes 86404
  205.4 40.9 %copy-start.16 = (f32[9,80,10]{1,2,0:T(8,128)S(1)}, f32[9,80,10]{1,2,0:T(8,128)}, u32[]{:S(2)}) copy-start(f32[9,80,10]{1,2,0:T(8,128)} %param.9) | copy-start | bytes 86404
Sparse Core Ops, SparseCore 0:
  141.3 29.9 all-gather.2
where the time goes:
time: 256 us; the launch traced here: 255 us
  blocking collectives  116 us (45%)
  waiting for transfers between devices  66.7 us (26%)
  starting transfers between devices  29.9 us (12%)
  local copies, waits for them, and re-layouts  16 us (6%)
  between operations  14.4 us (6%)
  matrix products  8.98 us (4%)
  other arithmetic  3.59 us (1%)
    all_gather x1, blocking collectives, per_device(): kernel = lax.all_gather(own, 'dp', axis=0, tiled=True)  92.6 us
    all_to_all x1, waiting for transfers between devices, per_device(): grad = lax.all_to_all(grad, 'dp', 0, 0, tiled=True)  39.4 us
    all_gather x1, waiting for transfers between devices, per_device(): err = lax.all_gather(error, 'rows', axis=1, tiled=True).reshape(-1, ch)  26.3 us
    all_to_all x1, blocking collectives, per_device(): part = lax.all_to_all(part, 'rows', 0, 0, tiled=True)  23 us
    all_to_all x1, starting transfers between devices, per_device(): grad = lax.all_to_all(grad, 'dp', 0, 0, tiled=True)  19.8 us
    all_to_all x1, starting transfers between devices, per_device(): x = lax.all_to_all(latents, 'rows', split_axis=3, concat_axis=1, tiled=True)  6.65 us
    unnamed x42, local copies, waits for them, and re-layouts  5.67 us
  transfers between devices with their start and end apart: 4, of which 3 were waited for; matrix products, arithmetic and copies ran while one was open for 4% of the time, Pallas kernels for 0%

commit v1 on v0

--- a/solution.py
+++ b/solution.py
@@ -2,6 +2,16 @@
 import jax.numpy as jnp
 from jax import lax
 from jax.sharding import PartitionSpec as P
+
+process_series_all = lambda x0: jnp.concatenate(
+    jax.lax.all_to_all(
+        jnp.stack(jax.lax.psum(1, "rows") * [x0], axis=0),
+        axis_name="rows",
+        split_axis=0,
+        concat_axis=0,
+    ),
+    axis=1,
+)
 
 
 def per_device(latents, target, weight, moment1, moment2):
@@ -24,7 +34,7 @@
     student = jnp.sum(part.astype(jnp.float32), axis=0).astype(jnp.bfloat16)
     error = student.astype(jnp.float32) - target.reshape(cells, ch).astype(jnp.float32)
     error = error.astype(jnp.bfloat16).reshape(batch, band, width, ch)
-    err = lax.all_gather(error, "rows", axis=1, tiled=True).reshape(-1, ch)
+    err = process_series_all(error).reshape(-1, ch)
     grad = lax.dot_general(err, x9, (((0,), (0,)), ((), ())), preferred_element_type=jnp.float32)
     grad = grad.astype(jnp.bfloat16).reshape(n_dp, ns, taps * cs)
     grad = lax.all_to_all(grad, "dp", 0, 0, tiled=True)

time: 256 us -> 221 us (0.86)
  between operations: 14.4 us -> 0.86 us
  waiting for transfers between devices: 66.7 us -> 57 us
  starting transfers between devices: 29.9 us -> 20.5 us
    all_gather x1 -> x0, waiting for transfers between devices: 26.3 us -> none  [per_device(): err = lax.all_gather(error, 'rows', axis=1, tiled=True).reshape(-1, ch)]
    all_to_all x0 -> x1, waiting for transfers between devices: none -> 16.5 us  [jax.lax.all_to_all(jnp.stack(jax.lax.psum(1, 'rows') * [x0], axis=0), axi...]
    all_to_all x1, starting transfers between devices: 19.8 us -> 6.1 us  [per_device(): grad = lax.all_to_all(grad, 'dp', 0, 0, tiled=True)]
    all_to_all x0 -> x1, starting transfers between devices: none -> 4.15 us  [jax.lax.all_to_all(jnp.stack(jax.lax.psum(1, 'rows') * [x0], axis=0), axi...]
    unnamed x42 -> x22, local copies, waits for them, and re-layouts: 5.67 us -> 5.62 us
  transfers between devices with their start and end apart: 4 -> 4, of which waited for: 3 -> 3; matrix products, arithmetic and copies ran while one was open for 4% -> 3% of each run, Pallas kernels for 0% -> 0%
where the time goes in v1:
time: 221 us; the launch traced here: 220 us
  blocking collectives  116 us (52%)
  waiting for transfers between devices  57 us (26%)
  starting transfers between devices  20.5 us (9%)
  local copies, waits for them, and re-layouts  16.9 us (8%)
  matrix products  7.04 us (3%)
    all_gather x1, blocking collectives, per_device(): kernel = lax.all_gather(own, 'dp', axis=0, tiled=True)  92.9 us
    all_to_all x1, waiting for transfers between devices, per_device(): grad = lax.all_to_all(grad, 'dp', 0, 0, tiled=True)  39.6 us
    all_to_all x1, blocking collectives, per_device(): part = lax.all_to_all(part, 'rows', 0, 0, tiled=True)  22.9 us
    all_to_all x1, waiting for transfers between devices, jax.lax.all_to_all(jnp.stack(jax.lax.psum(1, 'rows') * [x0], axis=0), axi...  16.5 us
    all_to_all x1, starting transfers between devices, per_device(): x = lax.all_to_all(latents, 'rows', split_axis=3, concat_axis=1, tiled=True)  6.65 us
    all_to_all x1, starting transfers between devices, per_device(): grad = lax.all_to_all(grad, 'dp', 0, 0, tiled=True)  6.1 us
    unnamed x22, local copies, waits for them, and re-layouts  5.62 us
  transfers between devices with their start and end apart: 4, of which 3 were waited for; matrix products, arithmetic and copies ran while one was open for 3% of the time, Pallas kernels for 0%

profile of v1, /device:TPU:1, one launch (start us, length us, event | category | flops | bytes accessed | tf_op | source)
XLA Modules:
  0.0 220.0 jit_solution(1507548681736204194)
XLA Ops:
  0.6 1.3 copy.33
  2.0 1.3 reshape.184
  3.3 6.6 %all-to-all-start = ((bf16[8,2,5120]{2,1,0:T(2,128)(2,1)}), bf16[8,2,5120]{2,1,0:T(2,128)(2,1)S(1)}, u32[]{:S(2)}, u32[]{:S(2)}) async-start(bf16[8,2,5120]{2,1,0:T(2,128)(2,1)} %reshape.184), calls=%async_computation | async-start | bytes 327680 | tf_op jit(solution)/shard_map/all_to_all | solution.py:26
  9.9 0.1 reshape.179
  10.0 92.9 %all-gather = bf16[64,10,720]{2,1,0:T(8,128)(2,1)S(1)} all-gather(bf16[1,10,720]{2,1,0:T(8,128)(2,1)S(1)} %reshape.179), channel_id=1, replica_groups=mesh['dp'=64,'rows'=8] {'dp'}, dimensions={0}, use_global_device_ids=true | all-gather | bytes 936000 | tf_op jit(solution)/shard_map/all_gather | solution.py:25
  103.0 0.6 reshape.180
  103.6 0.3 reshape.185
  103.9 0.4 copy.49
  104.4 1.4 pad_slice_fusion.8
  105.8 2.8 %concatenate.31 = bf16[1024,720]{1,0:T(8,128)(2,1)S(1)} concatenate(bf16[1024,80]{1,0:T(8,128)(2,1)} %bitcast.71, bf16[1024,80]{1,0:T(8,128)(2,1)S(1)} %bitcast.65, bf16[1024,80]{1,0:T(8,128)(2,1)} %bitcast.66, bf16[1024,80]{1,0:T(8,128)(2,1)} %bitcast.67, bf16[1024,80]{1,0:T(8,128)(2,1)S(1)} %bitcast.58, bf16[1024,80]{1,0:T(8,128)(2,1)} %bitcast.68, bf16[1024,80]{1,0:T(8,128)(2,1)} %bitcast.69, ...), dimensions={1} | concatenate | bytes 2949120 | tf_op jit(solution)/shard_map/concatenate | solution.py:29
  108.6 1.4 convolution_convert_fusion
  110.1 22.9 %all_to_all.51 = bf16[8,128,640]{2,1,0:T(8,128)(2,1)S(1)} all-to-all(bf16[8,128,640]{2,1,0:T(8,128)(2,1)S(1)} %bitcast.61), channel_id=1, replica_groups=mesh['dp'=64,'rows'=8] {'rows'}, dimensions={0} | all-to-all | bytes 2621440 | tf_op jit(solution)/shard_map/all_to_all | solution.py:33
  132.9 0.2 reduce_sum.21
  133.2 1.2 stack.3
  134.4 4.2 %all-to-all-start.2 = ((bf16[8,1,4,32,640]{4,3,2,1,0:T(8,128)(2,1)}), bf16[8,1,4,32,640]{4,3,2,1,0:T(8,128)(2,1)S(1)}, u32[]{:S(2)}, u32[]{:S(2)}) async-start(bf16[8,1,4,32,640]{4,3,2,1,0:T(8,128)(2,1)} %stack.3), calls=%async_computation.2 | async-start | bytes 2621440 | tf_op jit(solution)/shard_map/all_to_all | solution.py:7
  138.6 1.3 copy.38
  139.9 16.5 %all-to-all-done.2 = bf16[8,1,4,32,640]{4,3,2,1,0:T(8,128)(2,1)S(1)} async-done(((bf16[8,1,4,32,640]{4,3,2,1,0:T(8,128)(2,1)}), bf16[8,1,4,32,640]{4,3,2,1,0:T(8,128)(2,1)S(1)}, u32[]{:S(2)}, u32[]{:S(2)}) %all-to-all-start.2) | async-done | bytes 1310752 | tf_op jit(solution)/shard_map/all_to_all | solution.py:7
  156.3 3.3 %convolution_bitcast_fusion = f32[1,32,32,9,80]{4,2,3,1,0:T(8,128)S(1)} fusion(bf16[32,32,640,1]{2,1,3,0:T(8,128)(2,1)S(1)} %bitcast.59, bf16[9,80,640,1]{2,1,0,3:T(8,128)(2,1)} %bitcast.72), kind=kOutput, calls=%fused_computation.9 | convolution fusion | flops 943718400 | bytes 5181440 | tf_op jit(solution)/shard_map/dot_general | solution.py:43
  159.7 1.3 fusion.9
  161.0 3.7 %all-to-all-start.3 = ((bf16[1,32,32,80]{3,2,0,1:T(8,128)(2,1)}), bf16[1,32,32,80]{3,2,0,1:T(8,128)(2,1)S(1)}, u32[]{:S(2)}, u32[]{:S(2)}) async-start(bf16[1,32,32,80]{3,2,0,1:T(8,128)(2,1)} %fusion.9), calls=%async_computation.3 | async-start | bytes 524288 | tf_op jit(solution)/shard_map/all_to_all | solution.py:51
  164.6 2.3 %convolution_convert_fusion.1 = bf16[640,720]{0,1:T(8,128)(2,1)} fusion(bf16[1024,640]{1,0:T(8,128)(2,1)S(1)} %bitcast.60, bf16[1024,720]{1,0:T(8,128)(2,1)S(1)} %copy-done.1), kind=kOutput, calls=%fused_computation.11 | convolution fusion | flops 944179200 | bytes 3706880 | tf_op jit(solution)/shard_map/dot_general | solution.py:38
  166.9 1.6 copy.42
  168.5 1.4 reshape.173
  169.8 0.9 all-to-all-done.3
  170.8 6.1 %all-to-all-start.4 = ((bf16[64,10,720]{2,1,0:T(8,128)(2,1)}), bf16[64,10,720]{2,1,0:T(8,128)(2,1)S(1)}, u32[]{:S(2)}, u32[]{:S(2)}) async-start(bf16[64,10,720]{2,1,0:T(8,128)(2,1)} %reshape.173), calls=%async_computation.4 | async-start | bytes 3145728 | tf_op jit(solution)/shard_map/all_to_all | solution.py:40
  176.9 0.2 copy.40
  177.1 0.9 all_to_all.44
  178.0 39.6 %all-to-all-done.4 = bf16[64,10,720]{2,1,0:T(8,128)(2,1)S(1)} async-done(((bf16[64,10,720]{2,1,0:T(8,128)(2,1)}), bf16[64,10,720]{2,1,0:T(8,128)(2,1)S(1)}, u32[]{:S(2)}, u32[]{:S(2)}) %all-to-all-start.4) | async-done | bytes 921632 | tf_op jit(solution)/shard_map/all_to_all | solution.py:40
  217.5 0.3 convert_reduce_fusion
  218.0 0.6 copy.45
  218.7 0.6 copy.46
  219.3 0.6 copy.47
  (22 shorter events, 0.3 us)
Async XLA Ops:
  0.6 9.3 %copy-start.3 = (f32[9,80,10]{1,2,0:T(8,128)S(1)}, f32[9,80,10]{1,2,0:T(8,128)}, u32[]{:S(2)}) copy-start(f32[9,80,10]{1,2,0:T(8,128)} %param.7) | copy-start | bytes 86404
  3.3 100.3 %all-to-all-start = ((bf16[8,2,5120]{2,1,0:T(2,128)(2,1)}), bf16[8,2,5120]{2,1,0:T(2,128)(2,1)S(1)}, u32[]{:S(2)}, u32[]{:S(2)}) async-start(bf16[8,2,5120]{2,1,0:T(2,128)(2,1)} %reshape.184), calls=%async_computation | async-start | bytes 327680 | tf_op jit(solution)/shard_map/all_to_all | solution.py:26
  108.6 1.4 copy-start
  110.0 23.1 %copy-start.4 = (bf16[1,4,32,640]{3,2,1,0:T(8,128)(2,1)S(1)}, bf16[1,4,32,640]{3,2,1,0:T(8,128)(2,1)}, u32[]{:S(2)}) copy-start(bf16[1,4,32,640]{3,2,1,0:T(8,128)(2,1)} %param.6) | copy-start | bytes 491524
  133.1 1.3 copy-start.2
  134.4 21.9 %all-to-all-start.2 = ((bf16[8,1,4,32,640]{4,3,2,1,0:T(8,128)(2,1)}), bf16[8,1,4,32,640]{4,3,2,1,0:T(8,128)(2,1)S(1)}, u32[]{:S(2)}, u32[]{:S(2)}) async-start(bf16[8,1,4,32,640]{4,3,2,1,0:T(8,128)(2,1)} %stack.3), calls=%async_computation.2 | async-start | bytes 2621440 | tf_op jit(solution)/shard_map/all_to_all | solution.py:7
  159.7 4.9 %copy-start.1 = (bf16[1024,720]{1,0:T(8,128)(2,1)S(1)}, bf16[1024,720]{1,0:T(8,128)(2,1)}, u32[]{:S(2)}) copy-start(bf16[1024,720]{1,0:T(8,128)(2,1)} %copy-done) | copy-start | bytes 4423684
  161.0 9.8 %all-to-all-start.3 = ((bf16[1,32,32,80]{3,2,0,1:T(8,128)(2,1)}), bf16[1,32,32,80]{3,2,0,1:T(8,128)(2,1)S(1)}, u32[]{:S(2)}, u32[]{:S(2)}) async-start(bf16[1,32,32,80]{3,2,0,1:T(8,128)(2,1)} %fusion.9), calls=%async_computation.3 | async-start | bytes 524288 | tf_op jit(solution)/shard_map/all_to_all | solution.py:51
  170.8 46.7 %all-to-all-start.4 = ((bf16[64,10,720]{2,1,0:T(8,128)(2,1)}), bf16[64,10,720]{2,1,0:T(8,128)(2,1)S(1)}, u32[]{:S(2)}, u32[]{:S(2)}) async-start(bf16[64,10,720]{2,1,0:T(8,128)(2,1)} %reshape.173), calls=%async_computation.4 | async-start | bytes 3145728 | tf_op jit(solution)/shard_map/all_to_all | solution.py:40
  176.9 41.0 %copy-start.5 = (f32[9,80,10]{1,2,0:T(8,128)S(1)}, f32[9,80,10]{1,2,0:T(8,128)}, u32[]{:S(2)}) copy-start(f32[9,80,10]{1,2,0:T(8,128)} %param.8) | copy-start | bytes 86404
  176.9 41.0 %copy-start.6 = (f32[9,80,10]{1,2,0:T(8,128)S(1)}, f32[9,80,10]{1,2,0:T(8,128)}, u32[]{:S(2)}) copy-start(f32[9,80,10]{1,2,0:T(8,128)} %param.9) | copy-start | bytes 86404
